TPU v7x, 256 devices: a whole 4x4x8 slice. The times are simulated.
256 devices in a mesh: rows: 64 (over z, y, core), cols: 4 (over x).
Axes of the slice: x: 4, y: 4, z: 8, core: 2. Of those that a mesh axis runs over, the one named last changes fastest.
Arguments:
- feats_t: bfloat16 [128, 131072], P('cols', 'rows'), may hold values from -6 to 6
- adj_index: int32 [1024, 16], replicated, may hold values from 0 to 1023, as said below
- adj_weight: bfloat16 [1024, 16, 128, 128], P('rows'), as said below
- weight: bfloat16 [128, 256], replicated, may hold values from -0.5 to 0.5
- cotangent_t: bfloat16 [256, 131072], P('cols', 'rows'), may hold values from -6 to 6
Outputs:
- output_t: bfloat16 [256, 131072], P('cols', 'rows')
- weight_grad: float32 [128, 256], P('cols')
- feat_grad: float32 [128, 131072], P('cols', 'rows')
Inputs may be any that keep to these rules, and one draw needn't show every extreme that they name: `adj_index`: slot 0 of row block i names block i itself. Blocks are grouped 16 to a device in order. Slot 1 names a block of the next device (device index plus one, cyclically). The row blocks of one device name at most 4 distinct blocks of any other device, and exactly 4 of the next one. A block may stand in several slots of one row block. `adj_weight`: Nonnegative; about one entry in eight is nonzero.
All inputs are finite; a program needn't handle non-finite values.
Results may differ from a plain program's by a relative error of at most 0.0054.
Values may be sent and summed in bfloat16 or wider, within the bound.
A program may use at most 128 MiB of HBM per device.

v0:
```python
import math
import jax
import jax.numpy as jnp
from jax import lax
from jax.sharding import PartitionSpec as P


def body(feats_t, adj_index, adj_weight, weight, cotangent_t):
    feat_rows, node_cols = feats_t.shape
    blocks_n = adj_weight.shape[0]
    slots_n = adj_weight.shape[1]
    tile_n = adj_weight.shape[2]
    row_devs = lax.axis_size("rows")
    row_pos = lax.axis_index("rows")
    col_pos = lax.axis_index("cols")
    unit_rows = cotangent_t.shape[0]
    own_index = lax.dynamic_slice_in_dim(adj_index, row_pos * blocks_n, blocks_n, 0)
    own_flat = own_index.reshape(-1)
    local_tiles = feats_t.reshape(feat_rows, blocks_n, tile_n).transpose(1, 0, 2)
    whole_panel = lax.all_gather(local_tiles, "rows", axis=0, tiled=True)
    picked = whole_panel[own_index]
    aggregate = jnp.einsum("bkfj,bkij->fbi", picked, adj_weight, preferred_element_type=jnp.float32)
    aggregated = aggregate.reshape(feat_rows, node_cols).astype(jnp.bfloat16)
    w_slab = lax.dynamic_slice_in_dim(weight, col_pos * unit_rows, unit_rows, 1)
    pre_act = lax.dot_general(
        w_slab,
        lax.all_gather(aggregated, "cols", axis=0, tiled=True),
        (((0,), (0,)), ((), ())),
        preferred_element_type=jnp.float32,
    )
    output_t = jax.nn.silu(pre_act).astype(jnp.bfloat16)
    sigm = jax.nn.sigmoid(pre_act)
    pre_grad = (cotangent_t.astype(jnp.float32) * sigm * (1.0 + pre_act * (1.0 - sigm))).astype(
        jnp.bfloat16
    )
    w_mine = lax.dynamic_slice_in_dim(weight, col_pos * feat_rows, feat_rows, 0)
    portion = lax.all_gather(pre_grad, "cols", axis=0, tiled=True)
    grad_acc = jnp.dot(w_mine, portion, preferred_element_type=jnp.float32)
    block_grad = lax.dot_general(
        aggregated, portion, (((1,), (1,)), ((), ())), preferred_element_type=jnp.float32
    )
    grad_scale = 1.0 / math.sqrt(node_cols * row_devs)
    weight_grad = lax.psum(block_grad, "rows") * grad_scale
    agg_grad = grad_acc.astype(jnp.bfloat16)
    contrib = jnp.einsum(
        "fbi,bkij->bkfj",
        agg_grad.reshape(feat_rows, blocks_n, tile_n),
        adj_weight,
        preferred_element_type=jnp.float32,
    )
    contrib_flat = contrib.reshape(blocks_n * slots_n, feat_rows * tile_n)
    buffer = jax.ops.segment_sum(contrib_flat, own_flat, num_segments=row_devs * blocks_n)
    buffer = buffer.reshape(row_devs * blocks_n, feat_rows, tile_n)
    summed = lax.psum_scatter(buffer, "rows", scatter_dimension=0, tiled=True)
    feat_grad = summed.transpose(1, 0, 2).reshape(feat_rows, node_cols)
    return (output_t, weight_grad, feat_grad)


def solution(mesh):
    return jax.shard_map(
        body,
        mesh=mesh,
        in_specs=(P("cols", "rows"), P(), P("rows", None, None, None), P(), P("cols", "rows")),
        out_specs=(P("cols", "rows"), P("cols", None), P("cols", "rows")),
        check_vma=False,
    )
```

profile of v0, /device:TPU:4, one launch (start us, length us, event | category | flops | bytes accessed | tf_op | source)
XLA Modules:
  0.0 468.2 jit_solution(11323263088289372892)
XLA Ops:
  7.2 0.0 copy-start
  7.2 0.0 copy-start.3
  7.2 0.0 all-gather.3.cloned.1.call-start
  7.2 1.0 copy.36
  8.2 0.7 copy.22
  8.9 0.0 all-gather.3.cloned.1.call-update
  8.9 0.0 all-gather.5.cloned.1.call-start
  9.0 0.8 compare_select_fusion
  9.8 0.1 copy.23
  9.8 0.1 reshape.30
  9.9 87.4 %all-gather.3.cloned.1.call-done = bf16[1024,32,128]{2,1,0:T(8,128)(2,1)} async-done(((bf16[16,32,128]{2,1,0:T(8,128)(2,1)}), bf16[1024,32,128]{2,1,0:T(8,128)(2,1)}) %all-gather.3.cloned.1.call-update) | async-done | bytes 8388624 | tf_op jit(solution)/shard_map/all_gather | solution.py:20
  97.4 4.4 gather_fusion
  101.7 6.2 %fusion.5 = bf16[16,4,8,128]{3,2,1,0:T(8,128)(2,1)S(1)} fusion(bf16[16,16,32,128]{3,2,1,0:T(8,128)(2,1)S(1)} %bitcast.45, bf16[16,16,128,128]{3,2,1,0:T(8,128)(2,1)} %param.7), kind=kOutput, calls=%fused_computation.9 | convolution fusion | flops 268500992 | bytes 10616832 | tf_op jit(solution)/shard_map/bkfj,bkij->fbi/dot_general | solution.py:22
  108.0 11.6 %all_gather.10 = bf16[128,2048]{1,0:T(8,128)(2,1)S(1)} all-gather(bf16[32,2048]{1,0:T(8,128)(2,1)S(1)} %bitcast.47), channel_id=1, replica_groups=mesh['rows'=64,'cols'=4] {'cols'}, dimensions={0}, use_global_device_ids=true | all-gather | bytes 655360 | tf_op jit(solution)/shard_map/all_gather | solution.py:27
  119.5 0.0 copy-done
  119.5 0.0 copy-done.3
  119.5 1.3 multiply_convert_fusion
  120.8 0.0 all-gather.5.cloned.1.call-update
  120.9 0.2 reduce-scatter.2.cloned.1.call-start
  121.1 0.1 copy.25
  121.2 0.1 reshape.38
  121.3 24.2 %all-gather.5.cloned.1.call-done = bf16[256,2048]{1,0:T(8,128)(2,1)} async-done(((bf16[64,2048]{1,0:T(8,128)(2,1)}), bf16[256,2048]{1,0:T(8,128)(2,1)}) %all-gather.5.cloned.1.call-update) | async-done | bytes 1048592 | tf_op jit(solution)/shard_map/all_gather | solution.py:37
  145.5 1.5 fusion.6
  147.0 6.5 %fusion.7 = f32[16,32,16,128]{3,1,2,0:T(8,128)} fusion(bf16[16,16,128,128]{3,2,1,0:T(8,128)(2,1)} %param.7, bf16[32,16,128,1]{2,1,0,3:T(8,128)(2,1)S(1)} %bitcast.46), kind=kOutput, calls=%fused_computation.16 | convolution fusion | flops 268435456 | bytes 12713984 | tf_op jit(solution)/shard_map/fbi,bkij->bkfj/dot_general | solution.py:45
  153.6 16.7 %scatter_custom_fusion = f32[1024,4096]{1,0:T(8,128)} fusion(s32[256]{0:T(256)S(1)} %reshape.38, f32[]{:T(128)} %constant.11.clone.1, f32[32,8,32,128]{3,2,1,0:T(8,128)} %bitcast.44), kind=kCustom, calls=%fused_computation.2 | custom fusion | flops 1048576 | bytes 20971524 | tf_op jit(solution)/shard_map/scatter-add | solution.py:52
  170.3 17.5 %copy.27 = f32[1024,4096]{0,1:T(8,128)} copy(f32[1024,4096]{1,0:T(8,128)} %scatter_custom_fusion) | data formatting | bytes 33554432 | tf_op jit(solution)/shard_map/scatter-add | solution.py:52
  187.7 17.4 %copy.28 = f32[1024,32,128]{2,1,0:T(8,128)} copy(f32[1024,32,128]{0,2,1:T(8,128)} %bitcast.43) | data formatting | bytes 33554432 | tf_op jit(solution)/shard_map/reshape | solution.py:53
  205.1 0.0 copy-start.1
  205.1 0.0 copy-start.2
  205.1 0.0 reduce-scatter.2.cloned.1.call-update
  205.2 1.2 copy-done.2
  206.4 0.4 fusion.14
  206.8 252.5 %psum.7 = f32[32,256]{1,0:T(8,128)S(1)} all-reduce(f32[32,256]{1,0:T(8,128)S(1)} %fusion.14), channel_id=1, replica_groups=mesh['rows'=64,'cols'=4] {'rows'}, use_global_device_ids=true, to_apply=%region_0.1 | all-reduce | flops 8192 | bytes 65536 | tf_op jit(solution)/shard_map/psum | solution.py:43
  459.4 0.6 broadcast_multiply_fusion
  460.0 0.0 reduce-scatter.2.cloned.1.call-done
  460.0 1.7 copy_bitcast_fusion
  461.6 0.0 copy-done.1
  (3 shorter events, 0.1 us)
Async XLA Ops:
  7.2 112.4 %copy-start = (bf16[128,256]{1,0:T(8,128)(2,1)S(1)}, bf16[128,256]{1,0:T(8,128)(2,1)}, u32[]{:S(2)}) copy-start(bf16[128,256]{1,0:T(8,128)(2,1)} %param.8) | copy-start | bytes 196612
  7.2 112.4 %copy-start.3 = (bf16[64,2048]{1,0:T(8,128)(2,1)S(1)}, bf16[64,2048]{1,0:T(8,128)(2,1)}, u32[]{:S(2)}) copy-start(bf16[64,2048]{1,0:T(8,128)(2,1)} %param.9) | copy-start | bytes 786436
  7.2 90.2 %all-gather.3.cloned.1.call-start = ((), (), s32[]{:S(2)}) async-start(), calls=%async_computation.1 | async-start | bytes 8519680 | tf_op jit(solution)/shard_map/all_gather | solution.py:20
  8.9 136.6 %all-gather.5.cloned.1.call-start = ((), (), s32[]{:S(2)}) async-start(), calls=%async_computation.2 | async-start | bytes 1310720 | tf_op jit(solution)/shard_map/all_gather | solution.py:37
  120.9 339.1 %reduce-scatter.2.cloned.1.call-start = ((), (), s32[]{:S(2)}) async-start(), calls=%async_computation.3 | async-start | bytes 17039360 | tf_op jit(solution)/shard_map/reduce_scatter | solution.py:54
  205.1 256.5 %copy-start.1 = (bf16[128,256]{1,0:T(8,128)(2,1)S(1)}, bf16[128,256]{1,0:T(8,128)(2,1)}, u32[]{:S(2)}) copy-start(bf16[128,256]{1,0:T(8,128)(2,1)} %param.8) | copy-start | bytes 196612
  205.1 1.3 copy-start.2
Sparse Core Ops, SparseCore 0:
  11.4 85.9 all-gather.2
  121.0 24.4 all-gather.4
  205.3 191.1 reduce-scatter.1
where the time goes:
time: 469 us; the launch traced here: 468 us
  blocking collectives  264 us (56%)
  waiting for transfers between devices  112 us (24%)
  local copies, waits for them, and re-layouts  44.2 us (9%)
  other arithmetic  18.1 us (4%)
  matrix products  15.9 us (3%)
  between operations  13.8 us (3%)
    psum x1, blocking collectives, body(): weight_grad = lax.psum(block_grad, 'rows') * grad_scale  253 us
    all_gather x1, waiting for transfers between devices, body(): whole_panel = lax.all_gather(local_tiles, 'rows', axis=0, tiled=True)  87.4 us
    all_gather x1, waiting for transfers between devices, body(): portion = lax.all_gather(pre_grad, 'cols', axis=0, tiled=True)  24.2 us
    scatter-add x1, local copies, waits for them, and re-layouts, body(): jax.ops.segment_sum(contrib_flat, own_flat, num_segments=row_devs * block...  17.5 us
    reshape x1, local copies, waits for them, and re-layouts, body(): buffer = buffer.reshape(row_devs * blocks_n, feat_rows, tile_n)  17.4 us
    scatter-add x1, other arithmetic, body(): jax.ops.segment_sum(contrib_flat, own_flat, num_segments=row_devs * block...  16.7 us
    all_gather x1, blocking collectives, body(): lax.all_gather(aggregated, 'cols', axis=0, tiled=True)  11.6 us
  transfers between devices with their start and end apart: 3, of which 2 were waited for; matrix products, arithmetic and copies ran while one was open for 0% of the time, Pallas kernels for 0%

commit v1 on v0

--- a/solution.py
+++ b/solution.py
@@ -40,7 +40,7 @@
         aggregated, portion, (((1,), (1,)), ((), ())), preferred_element_type=jnp.float32
     )
     grad_scale = 1.0 / math.sqrt(node_cols * row_devs)
-    weight_grad = lax.psum(block_grad, "rows") * grad_scale
+    weight_grad = jnp.sum(lax.all_gather(block_grad, "rows"), axis=0) * grad_scale
     agg_grad = grad_acc.astype(jnp.bfloat16)
     contrib = jnp.einsum(
         "fbi,bkij->bkfj",

time: 469 us -> 428 us (0.913)
  blocking collectives: 264 us -> 11.6 us
  waiting for transfers between devices: 112 us -> 321 us
    psum x1 -> x0, blocking collectives: 253 us -> none  [body(): weight_grad = lax.psum(block_grad, 'rows') * grad_scale]
    reduce_scatter x1, waiting for transfers between devices: 0.01 us -> 189 us  [body(): summed = lax.psum_scatter(buffer, 'rows', scatter_dimension=0, tiled=True)]
    all_gather x0 -> x1, waiting for transfers between devices: none -> 19.6 us  [body(): lax.all_gather(block_grad, 'rows')]
  transfers between devices with their start and end apart: 3 -> 4, of which waited for: 2 -> 4; matrix products, arithmetic and copies ran while one was open for 0% -> 15% of each run, Pallas kernels for 0% -> 0%
where the time goes in v1:
time: 428 us; the launch traced here: 427 us
  waiting for transfers between devices  321 us (75%)
  local copies, waits for them, and re-layouts  43 us (10%)
  other arithmetic  19.8 us (5%)
  matrix products  17.8 us (4%)
  between operations  13.8 us (3%)
  blocking collectives  11.6 us (3%)
    reduce_scatter x1, waiting for transfers between devices, body(): summed = lax.psum_scatter(buffer, 'rows', scatter_dimension=0, tiled=True)  189 us
    all_gather x1, waiting for transfers between devices, body(): whole_panel = lax.all_gather(local_tiles, 'rows', axis=0, tiled=True)  87.4 us
    all_gather x1, waiting for transfers between devices, body(): portion = lax.all_gather(pre_grad, 'cols', axis=0, tiled=True)  24.6 us
    all_gather x1, waiting for transfers between devices, body(): lax.all_gather(block_grad, 'rows')  19.6 us
    scatter-add x1, local copies, waits for them, and re-layouts, body(): jax.ops.segment_sum(contrib_flat, own_flat, num_segments=row_devs * block...  17.5 us
    reshape x1, local copies, waits for them, and re-layouts, body(): buffer = buffer.reshape(row_devs * blocks_n, feat_rows, tile_n)  17.4 us
    scatter-add x1, other arithmetic, body(): jax.ops.segment_sum(contrib_flat, own_flat, num_segments=row_devs * block...  16.7 us
    all_gather x1, blocking collectives, body(): lax.all_gather(aggregated, 'cols', axis=0, tiled=True)  11.6 us
  transfers between devices with their start and end apart: 4, of which 4 were waited for; matrix products, arithmetic and copies ran while one was open for 15% of the time, Pallas kernels for 0%

profile of v1, /device:TPU:4, one launch (start us, length us, event | category | flops | bytes accessed | tf_op | source)
XLA Modules:
  0.0 427.1 jit_solution(18391385494839947578)
XLA Ops:
  7.2 0.0 copy-start
  7.2 0.0 copy-start.2
  7.2 0.0 all-gather.5.cloned.1.call-start
  7.2 1.0 copy.36
  8.2 0.7 copy.22
  8.9 0.0 all-gather.5.cloned.1.call-update
  8.9 0.0 all-gather.7.cloned.1.call-start
  9.0 0.8 compare_select_fusion
  9.8 0.1 copy.23
  9.8 0.1 reshape.30
  9.9 87.4 %all-gather.5.cloned.1.call-done = bf16[1024,32,128]{2,1,0:T(8,128)(2,1)} async-done(((bf16[16,32,128]{2,1,0:T(8,128)(2,1)}), bf16[1024,32,128]{2,1,0:T(8,128)(2,1)}) %all-gather.5.cloned.1.call-update) | async-done | bytes 8388624 | tf_op jit(solution)/shard_map/all_gather | solution.py:20
  97.4 4.4 %gather_fusion = bf16[256,32,128]{2,1,0:T(8,128)(2,1)S(1)} fusion(bf16[1024,32,128]{2,1,0:T(8,128)(2,1)} %all-gather.5.cloned.1.call-done, s32[1024]{0:T(1024)S(1)} %pad_clamp_fusion), kind=kCustom, calls=%fused_computation | custom fusion | bytes 4195328 | tf_op jit(solution)/shard_map/gather | solution.py:21
  101.7 6.2 %fusion.5 = bf16[16,4,8,128]{3,2,1,0:T(8,128)(2,1)S(1)} fusion(bf16[16,16,32,128]{3,2,1,0:T(8,128)(2,1)S(1)} %bitcast.46, bf16[16,16,128,128]{3,2,1,0:T(8,128)(2,1)} %param.7), kind=kOutput, calls=%fused_computation.9 | convolution fusion | flops 268500992 | bytes 10616832 | tf_op jit(solution)/shard_map/bkfj,bkij->fbi/dot_general | solution.py:22
  108.0 11.6 %all_gather.16 = bf16[128,2048]{1,0:T(8,128)(2,1)S(1)} all-gather(bf16[32,2048]{1,0:T(8,128)(2,1)S(1)} %bitcast.49), channel_id=1, replica_groups=mesh['rows'=64,'cols'=4] {'cols'}, dimensions={0}, use_global_device_ids=true | all-gather | bytes 655360 | tf_op jit(solution)/shard_map/all_gather | solution.py:27
  119.5 0.0 copy-done
  119.5 0.0 copy-done.2
  119.5 1.3 multiply_convert_fusion
  120.8 0.0 all-gather.7.cloned.1.call-update
  120.9 0.0 all-gather.9.cloned.1.call-start
  120.9 24.6 %all-gather.7.cloned.1.call-done = bf16[256,2048]{1,0:T(8,128)(2,1)} async-done(((bf16[64,2048]{1,0:T(8,128)(2,1)}), bf16[256,2048]{1,0:T(8,128)(2,1)}) %all-gather.7.cloned.1.call-update) | async-done | bytes 1048592 | tf_op jit(solution)/shard_map/all_gather | solution.py:37
  145.5 2.3 fusion.14
  147.8 0.0 all-gather.9.cloned.1.call-update
  147.8 0.2 reduce-scatter.2.cloned.1.call-start
  148.0 0.1 copy.25
  148.1 0.1 reshape.38
  148.2 1.5 fusion.6
  149.7 6.5 %fusion.7 = f32[16,32,16,128]{3,1,2,0:T(8,128)} fusion(bf16[16,16,128,128]{3,2,1,0:T(8,128)(2,1)} %param.7, bf16[32,16,128,1]{2,1,0,3:T(8,128)(2,1)S(1)} %bitcast.48), kind=kOutput, calls=%fused_computation.16 | convolution fusion | flops 268435456 | bytes 12713984 | tf_op jit(solution)/shard_map/fbi,bkij->bkfj/dot_general | solution.py:45
  156.3 16.7 %scatter_custom_fusion = f32[1024,4096]{1,0:T(8,128)} fusion(s32[256]{0:T(256)S(1)} %reshape.38, f32[]{:T(128)} %constant.9.clone.1, f32[32,8,32,128]{3,2,1,0:T(8,128)} %bitcast.45), kind=kCustom, calls=%fused_computation.2 | custom fusion | flops 1048576 | bytes 20971524 | tf_op jit(solution)/shard_map/scatter-add | solution.py:52
  172.9 17.5 %copy.27 = f32[1024,4096]{0,1:T(8,128)} copy(f32[1024,4096]{1,0:T(8,128)} %scatter_custom_fusion) | data formatting | bytes 33554432 | tf_op jit(solution)/shard_map/scatter-add | solution.py:52
  190.4 17.4 %copy.28 = f32[1024,32,128]{2,1,0:T(8,128)} copy(f32[1024,32,128]{0,2,1:T(8,128)} %bitcast.44) | data formatting | bytes 33554432 | tf_op jit(solution)/shard_map/reshape | solution.py:53
  207.8 0.0 copy-start.1
  207.8 0.0 reduce-scatter.2.cloned.1.call-update
  207.9 19.6 %all-gather.9.cloned.1.call-done = f32[2048,256]{1,0:T(8,128)} async-done(((f32[32,256]{1,0:T(8,128)}), f32[2048,256]{1,0:T(8,128)}) %all-gather.9.cloned.1.call-update) | async-done | bytes 2097168 | tf_op jit(solution)/shard_map/all_gather | solution.py:43
  227.5 1.7 reduce_sum.9
  229.2 0.6 broadcast_multiply_fusion
  229.8 189.0 %reduce-scatter.2.cloned.1.call-done = f32[16,32,128]{2,1,0:T(8,128)} async-done(((f32[1024,32,128]{2,1,0:T(8,128)}), f32[16,32,128]{2,1,0:T(8,128)}) %reduce-scatter.2.cloned.1.call-update) | async-done | bytes 262160 | tf_op jit(solution)/shard_map/reduce_scatter | solution.py:54
  418.9 1.7 copy_bitcast_fusion
  420.5 0.0 copy-done.1
  (3 shorter events, 0.1 us)
Async XLA Ops:
  7.2 112.4 %copy-start = (bf16[128,256]{1,0:T(8,128)(2,1)S(1)}, bf16[128,256]{1,0:T(8,128)(2,1)}, u32[]{:S(2)}) copy-start(bf16[128,256]{1,0:T(8,128)(2,1)} %param.8) | copy-start | bytes 196612
  7.2 112.4 %copy-start.2 = (bf16[64,2048]{1,0:T(8,128)(2,1)S(1)}, bf16[64,2048]{1,0:T(8,128)(2,1)}, u32[]{:S(2)}) copy-start(bf16[64,2048]{1,0:T(8,128)(2,1)} %param.9) | copy-start | bytes 786436
  7.2 90.2 %all-gather.5.cloned.1.call-start = ((), (), s32[]{:S(2)}) async-start(), calls=%async_computation.1 | async-start | bytes 8519680 | tf_op jit(solution)/shard_map/all_gather | solution.py:20
  8.9 136.6 %all-gather.7.cloned.1.call-start = ((), (), s32[]{:S(2)}) async-start(), calls=%async_computation.2 | async-start | bytes 1310720 | tf_op jit(solution)/shard_map/all_gather | solution.py:37
  120.9 106.6 %all-gather.9.cloned.1.call-start = ((), (), s32[]{:S(2)}) async-start(), calls=%async_computation.4 | async-start | bytes 2129920 | tf_op jit(solution)/shard_map/all_gather | solution.py:43
  147.8 271.1 %reduce-scatter.2.cloned.1.call-start = ((), (), s32[]{:S(2)}) async-start(), calls=%async_computation.3 | async-start | bytes 17039360 | tf_op jit(solution)/shard_map/reduce_scatter | solution.py:54
  207.8 212.7 %copy-start.1 = (bf16[128,256]{1,0:T(8,128)(2,1)S(1)}, bf16[128,256]{1,0:T(8,128)(2,1)}, u32[]{:S(2)}) copy-start(bf16[128,256]{1,0:T(8,128)(2,1)} %param.8) | copy-start | bytes 196612
Sparse Core Ops, SparseCore 0:
  11.4 85.9 all-gather.4
  121.0 24.4 all-gather.6
  148.8 78.5 all-gather.8
  231.8 187.0 reduce-scatter.1
